TPU v7x, 256 devices: a whole 4x4x8 slice. The times are simulated.
256 devices in a mesh: dp: 2 (over core), seq: 8 (over z), expert: 16 (over y, x).
Axes of the slice: x: 4, y: 4, z: 8, core: 2. Of those that a mesh axis runs over, the one named last changes fastest.
Arguments:
- tokens: bfloat16 [16384, 2048], P(('dp', 'seq')), may hold values from -6 to 6
- phi: bfloat16 [2048, 32], P(None, 'expert'), may hold values from -40 to 40
- w_in: bfloat16 [32, 2048, 8192], P('expert', None, ('dp', 'seq')), may hold values from -1 to 1
- w_out: bfloat16 [32, 8192, 2048], P('expert', ('dp', 'seq')), may hold values from -0.25 to 0.25
Outputs:
- mixed: bfloat16 [16384, 2048], P(('dp', 'seq', 'expert'))
All inputs are finite; a program needn't handle non-finite values.
Results may differ from a plain program's by a relative error of at most 0.0068.
Values may be sent and summed in bfloat16 or wider, within the bound.
A program may use at most 64 MiB of HBM per device.

v0:
```python
import jax
import jax.numpy as jnp
from jax import lax
from jax.sharding import PartitionSpec as P


def on_device(tokens, phi, w_in, w_out):
    n_expert = lax.axis_size("expert")
    rows_out = tokens.shape[0] // n_expert
    phi_all = lax.all_gather(phi, "expert", axis=1, tiled=True)
    logits = lax.dot_general(
        phi, tokens, (((0,), (1,)), ((), ())), preferred_element_type=jnp.float32
    )
    slot_max = lax.pmax(jnp.max(logits, axis=1), "seq")
    spread = jnp.exp(logits - slot_max[:, None])
    numerator = jnp.dot(spread.astype(jnp.bfloat16), tokens, preferred_element_type=jnp.float32)
    denominator = jnp.sum(spread, axis=1)
    numer_seq, denom_seq = lax.psum((numerator, denominator), "seq")
    own_slots = (numer_seq / denom_seq[:, None]).astype(jnp.bfloat16)
    slot_in = lax.all_gather(own_slots[None], "dp", axis=0, tiled=True)
    hidden = jax.nn.gelu(
        jnp.einsum("ced,edf->cef", slot_in, w_in, preferred_element_type=jnp.float32),
        approximate=True,
    ).astype(jnp.bfloat16)
    partial_value = jnp.einsum("cef,efd->ced", hidden, w_out, preferred_element_type=jnp.float32)
    totals = lax.psum(partial_value, ("dp", "seq"))
    summed = lax.dynamic_index_in_dim(totals, lax.axis_index("dp"), 0, keepdims=False)
    slot_out = lax.all_gather(summed.astype(jnp.bfloat16), "expert", axis=0, tiled=True)
    rows = lax.dynamic_slice_in_dim(tokens, lax.axis_index("expert") * rows_out, rows_out, 0)
    row_logits = lax.dot_general(
        phi_all, rows, (((0,), (1,)), ((), ())), preferred_element_type=jnp.float32
    )
    row_max = jnp.max(row_logits, axis=0)
    combine_weights = jnp.exp(row_logits - row_max[None, :])
    mixed_numer = lax.dot_general(
        combine_weights.astype(jnp.bfloat16),
        slot_out,
        (((0,), (0,)), ((), ())),
        preferred_element_type=jnp.float32,
    )
    mixed_denom = jnp.sum(combine_weights, axis=0)
    return (mixed_numer / mixed_denom[:, None]).astype(jnp.bfloat16)


def solution(mesh):
    placed = (
        P(("dp", "seq"), None),
        P(None, "expert"),
        P("expert", None, ("dp", "seq")),
        P("expert", ("dp", "seq"), None),
    )
    return jax.shard_map(
        on_device,
        mesh=mesh,
        in_specs=placed,
        out_specs=P(("dp", "seq", "expert"), None),
        check_vma=False,
    )
```

profile of v0, /device:TPU:32, one launch (start us, length us, event | category | flops | bytes accessed | tf_op | source)
XLA Modules:
  0.0 159.4 jit_solution(6288700102996713554)
XLA Ops:
  0.0 3.5 %fusion.39 = (f32[2]{0:T(128)S(1)}, f32[2,1024]{1,0:T(2,128)S(1)}) fusion(bf16[2048,2]{0,1:T(2,128)(2,1)} %param.5, bf16[1024,2048]{1,0:T(8,128)(2,1)} %param.4), kind=kOutput, calls=%fused_computation.39 | convolution fusion | flops 8390654 | bytes 4210696 | tf_op jit(solution)/shard_map/dot_general | solution.py:11
  3.5 17.9 %pmax.7 = f32[2]{0:T(128)S(1)} all-reduce(f32[2]{0:T(128)S(1)} %get-tuple-element.9), channel_id=1, replica_groups=mesh['dp'=2,'seq'=8,'expert'=16] {'seq'}, use_global_device_ids=true, to_apply=%region_2.0 | all-reduce | flops 2 | bytes 16 | tf_op jit(solution)/shard_map/pmax | solution.py:14
  21.4 0.2 fusion.25
  21.6 2.9 %fusion.27 = f32[2,2048]{1,0:T(2,128)S(1)} fusion(bf16[1024,2048]{1,0:T(8,128)(2,1)} %param.4, f32[2,1024]{1,0:T(2,128)S(1)} %get-tuple-element.10, f32[2]{0:T(128)S(1)} %pmax.7), kind=kOutput, calls=%fused_computation.28 | convolution fusion | flops 8392704 | bytes 4218888 | tf_op jit(solution)/shard_map/dot_general | solution.py:16
  24.5 27.9 %all-reduce = (f32[2,2048]{1,0:T(2,128)S(1)}, f32[2]{0:T(128)S(1)}) all-reduce(f32[2,2048]{1,0:T(2,128)S(1)} %fusion.27, f32[2]{0:T(128)S(1)} %fusion.25), channel_id=1, replica_groups=mesh['dp'=2,'seq'=8,'expert'=16] {'seq'}, use_global_device_ids=true, to_apply=%region_3.0 | all-reduce | flops 4098 | bytes 32784 | tf_op jit(solution)/shard_map/psum | solution.py:18
  52.4 0.1 fusion.24
  52.5 1.8 %all-gather.3 = bf16[2,2,2048]{2,1,0:T(2,128)(2,1)S(1)} all-gather(bf16[1,2,2048]{2,1,0:T(2,128)(2,1)S(1)} %fusion.24), channel_id=2, replica_groups=mesh['dp'=2,'seq'=8,'expert'=16] {'dp'}, dimensions={0}, use_global_device_ids=true | all-gather | bytes 24576 | tf_op jit(solution)/shard_map/all_gather | solution.py:20
  54.3 0.0 copy-start
  54.3 4.7 %convolution_bitcast_fusion = f32[2,2,2048]{2,0,1:T(2,128)S(1)} fusion(bf16[2,512,2048]{2,1,0:T(8,128)(2,1)} %param.7, bf16[2,2048,512]{2,1,0:T(8,128)(2,1)} %param.6, bf16[2,2,2048]{2,1,0:T(2,128)(2,1)S(1)} %all-gather.3), kind=kOutput, calls=%fused_computation.2 | convolution fusion | flops 16795648 | bytes 8437760 | tf_op jit(solution)/shard_map/cef,efd->ced/dot_general | solution.py:25
  59.0 51.1 %psum.23 = bf16[2,2,2048]{2,0,1:T(2,128)(2,1)S(1)} all-reduce(f32[2,2,2048]{2,0,1:T(2,128)S(1)} %convolution_bitcast_fusion), channel_id=1, replica_groups=mesh['dp'=2,'seq'=8,'expert'=16] {'dp','seq'}, use_global_device_ids=true, to_apply=%region_6.7 | all-reduce | flops 8192 | bytes 49152 | tf_op jit(solution)/shard_map/psum | solution.py:26
  110.1 0.0 copy-done
  110.1 24.0 %all-gather.2 = bf16[16,2,2048]{2,1,0:T(2,128)(2,1)S(1)} all-gather(bf16[1,2,2048]{2,1,0:T(2,128)(2,1)S(1)} %bitcast.24), channel_id=1, replica_groups=mesh['dp'=2,'seq'=8,'expert'=16] {'expert'}, dimensions={0}, use_global_device_ids=true | all-gather | bytes 139264 | tf_op jit(solution)/shard_map/all_gather | solution.py:10
  134.1 0.1 reshape.8
  134.1 1.2 fusion.38
  135.3 23.1 %all-gather.1 = bf16[1,32,2048]{2,0,1:T(2,128)(2,1)S(1)} all-gather(bf16[1,2,2048]{2,0,1:T(2,128)(2,1)S(1)} %dynamic-slice_convert_fusion), channel_id=3, replica_groups=mesh['dp'=2,'seq'=8,'expert'=16] {'expert'}, dimensions={1}, use_global_device_ids=true | all-gather | bytes 139264 | tf_op jit(solution)/shard_map/all_gather | solution.py:28
  158.4 1.0 fusion
  (2 shorter events, 0.1 us)
Async XLA Ops:
  54.3 55.8 %copy-start = (bf16[2048,2]{0,1:T(2,128)(2,1)S(1)}, bf16[2048,2]{0,1:T(2,128)(2,1)}, u32[]{:S(2)}) copy-start(bf16[2048,2]{0,1:T(2,128)(2,1)} %param.5) | copy-start | bytes 24580
where the time goes:
time: 160 us; the launch traced here: 159 us
  blocking collectives  146 us (91%)
  matrix products  13.2 us (8%)
    psum x1, blocking collectives, on_device(): totals = lax.psum(partial_value, ('dp', 'seq'))  51.1 us
    psum x1, blocking collectives, on_device(): numer_seq, denom_seq = lax.psum((numerator, denominator), 'seq')  27.9 us
    all_gather x1, blocking collectives, on_device(): phi_all = lax.all_gather(phi, 'expert', axis=1, tiled=True)  24 us
    all_gather x1, blocking collectives, on_device(): lax.all_gather(summed.astype(jnp.bfloat16), 'expert', axis=0, tiled=True)  23.1 us
    pmax x1, blocking collectives, on_device(): slot_max = lax.pmax(jnp.max(logits, axis=1), 'seq')  17.9 us
    dot_general x1, matrix products, on_device(): jnp.einsum('cef,efd->ced', hidden, w_out, preferred_element_type=jnp.floa...  4.66 us
    dot_general x1, matrix products, on_device(): lax.dot_general(phi, tokens, (((0,), (1,)), ((), ())), preferred_element_...  3.5 us

commit v1 on v0

--- a/solution.py
+++ b/solution.py
@@ -23,7 +23,7 @@
         approximate=True,
     ).astype(jnp.bfloat16)
     partial_value = jnp.einsum("cef,efd->ced", hidden, w_out, preferred_element_type=jnp.float32)
-    totals = lax.psum(partial_value, ("dp", "seq"))
+    totals = lax.psum(lax.psum(partial_value, "seq"), "dp")
     summed = lax.dynamic_index_in_dim(totals, lax.axis_index("dp"), 0, keepdims=False)
     slot_out = lax.all_gather(summed.astype(jnp.bfloat16), "expert", axis=0, tiled=True)
     rows = lax.dynamic_slice_in_dim(tokens, lax.axis_index("expert") * rows_out, rows_out, 0)

time: 160 us -> 140 us (0.88)
  blocking collectives: 146 us -> 125 us
    psum x1 -> x2, blocking collectives: 51.1 us -> 30.4 us  [on_device(): totals = lax.psum(lax.psum(partial_value, 'seq'), 'dp')]
where the time goes in v1:
time: 140 us; the launch traced here: 139 us
  blocking collectives  125 us (89%)
  matrix products  13.2 us (9%)
    psum x2, blocking collectives, on_device(): totals = lax.psum(lax.psum(partial_value, 'seq'), 'dp')  30.4 us
    psum x1, blocking collectives, on_device(): numer_seq, denom_seq = lax.psum((numerator, denominator), 'seq')  27.9 us
    all_gather x1, blocking collectives, on_device(): phi_all = lax.all_gather(phi, 'expert', axis=1, tiled=True)  23.9 us
    all_gather x1, blocking collectives, on_device(): lax.all_gather(summed.astype(jnp.bfloat16), 'expert', axis=0, tiled=True)  23.1 us
    pmax x1, blocking collectives, on_device(): slot_max = lax.pmax(jnp.max(logits, axis=1), 'seq')  17.9 us
    dot_general x1, matrix products, on_device(): jnp.einsum('cef,efd->ced', hidden, w_out, preferred_element_type=jnp.floa...  4.66 us
    dot_general x1, matrix products, on_device(): lax.dot_general(phi, tokens, (((0,), (1,)), ((), ())), preferred_element_...  3.5 us
    dot_general x1, matrix products, on_device(): jnp.dot(spread.astype(jnp.bfloat16), tokens, preferred_element_type=jnp.f...  2.88 us

profile of v1, /device:TPU:32, one launch (start us, length us, event | category | flops | bytes accessed | tf_op | source)
XLA Modules:
  0.0 138.7 jit_solution(14545192414172696915)
XLA Ops:
  0.0 3.5 %fusion.39 = (f32[2]{0:T(128)S(1)}, f32[2,1024]{1,0:T(2,128)S(1)}) fusion(bf16[2048,2]{0,1:T(2,128)(2,1)} %param.5, bf16[1024,2048]{1,0:T(8,128)(2,1)} %param.4), kind=kOutput, calls=%fused_computation.39 | convolution fusion | flops 8390654 | bytes 4210696 | tf_op jit(solution)/shard_map/dot_general | solution.py:11
  3.5 17.9 %pmax.7 = f32[2]{0:T(128)S(1)} all-reduce(f32[2]{0:T(128)S(1)} %get-tuple-element.9), channel_id=1, replica_groups=mesh['dp'=2,'seq'=8,'expert'=16] {'seq'}, use_global_device_ids=true, to_apply=%region_2.0 | all-reduce | flops 2 | bytes 16 | tf_op jit(solution)/shard_map/pmax | solution.py:14
  21.4 0.2 fusion.25
  21.6 2.9 %fusion.27 = f32[2,2048]{1,0:T(2,128)S(1)} fusion(bf16[1024,2048]{1,0:T(8,128)(2,1)} %param.4, f32[2,1024]{1,0:T(2,128)S(1)} %get-tuple-element.10, f32[2]{0:T(128)S(1)} %pmax.7), kind=kOutput, calls=%fused_computation.28 | convolution fusion | flops 8392704 | bytes 4218888 | tf_op jit(solution)/shard_map/dot_general | solution.py:16
  24.5 27.9 %all-reduce = (f32[2,2048]{1,0:T(2,128)S(1)}, f32[2]{0:T(128)S(1)}) all-reduce(f32[2,2048]{1,0:T(2,128)S(1)} %fusion.27, f32[2]{0:T(128)S(1)} %fusion.25), channel_id=1, replica_groups=mesh['dp'=2,'seq'=8,'expert'=16] {'seq'}, use_global_device_ids=true, to_apply=%region_3.0 | all-reduce | flops 4098 | bytes 32784 | tf_op jit(solution)/shard_map/psum | solution.py:18
  52.4 0.1 fusion.24
  52.5 1.8 %all-gather.3 = bf16[2,2,2048]{2,1,0:T(2,128)(2,1)S(1)} all-gather(bf16[1,2,2048]{2,1,0:T(2,128)(2,1)S(1)} %fusion.24), channel_id=2, replica_groups=mesh['dp'=2,'seq'=8,'expert'=16] {'dp'}, dimensions={0}, use_global_device_ids=true | all-gather | bytes 24576 | tf_op jit(solution)/shard_map/all_gather | solution.py:20
  54.3 0.0 copy-start
  54.3 4.7 %convolution_bitcast_fusion = f32[2,2,2048]{2,0,1:T(2,128)S(1)} fusion(bf16[2,512,2048]{2,1,0:T(8,128)(2,1)} %param.7, bf16[2,2048,512]{2,1,0:T(8,128)(2,1)} %param.6, bf16[2,2,2048]{2,1,0:T(2,128)(2,1)S(1)} %all-gather.3), kind=kOutput, calls=%fused_computation.2 | convolution fusion | flops 16795648 | bytes 8437760 | tf_op jit(solution)/shard_map/cef,efd->ced/dot_general | solution.py:25
  59.0 27.0 %psum.30 = f32[2,2,2048]{2,0,1:T(2,128)S(1)} all-reduce(f32[2,2,2048]{2,0,1:T(2,128)S(1)} %convolution_bitcast_fusion), channel_id=1, replica_groups=mesh['dp'=2,'seq'=8,'expert'=16] {'seq'}, use_global_device_ids=true, to_apply=%region_6.0 | all-reduce | flops 8192 | bytes 65536 | tf_op jit(solution)/shard_map/psum | solution.py:26
  86.0 3.4 %psum.31 = bf16[2,2,2048]{2,0,1:T(2,128)(2,1)S(1)} all-reduce(f32[2,2,2048]{2,0,1:T(2,128)S(1)} %psum.30), channel_id=1, replica_groups=mesh['dp'=2,'seq'=8,'expert'=16] {'dp'}, use_global_device_ids=true, to_apply=%region_7.8 | all-reduce | flops 8192 | bytes 49152 | tf_op jit(solution)/shard_map/psum | solution.py:26
  89.4 0.0 copy-done
  89.5 23.9 %all-gather.2 = bf16[16,2,2048]{2,1,0:T(2,128)(2,1)S(1)} all-gather(bf16[1,2,2048]{2,1,0:T(2,128)(2,1)S(1)} %bitcast.24), channel_id=1, replica_groups=mesh['dp'=2,'seq'=8,'expert'=16] {'expert'}, dimensions={0}, use_global_device_ids=true | all-gather | bytes 139264 | tf_op jit(solution)/shard_map/all_gather | solution.py:10
  113.4 0.1 reshape.8
  113.5 1.2 fusion.38
  114.7 23.1 %all-gather.1 = bf16[1,32,2048]{2,0,1:T(2,128)(2,1)S(1)} all-gather(bf16[1,2,2048]{2,0,1:T(2,128)(2,1)S(1)} %dynamic-slice_convert_fusion), channel_id=3, replica_groups=mesh['dp'=2,'seq'=8,'expert'=16] {'expert'}, dimensions={1}, use_global_device_ids=true | all-gather | bytes 139264 | tf_op jit(solution)/shard_map/all_gather | solution.py:28
  137.8 1.0 fusion
  (2 shorter events, 0.1 us)
Async XLA Ops:
  54.3 35.1 %copy-start = (bf16[2048,2]{0,1:T(2,128)(2,1)S(1)}, bf16[2048,2]{0,1:T(2,128)(2,1)}, u32[]{:S(2)}) copy-start(bf16[2048,2]{0,1:T(2,128)(2,1)} %param.5) | copy-start | bytes 24580

commit v2 on v0

--- a/solution.py
+++ b/solution.py
@@ -7,7 +7,11 @@
 def on_device(tokens, phi, w_in, w_out):
     n_expert = lax.axis_size("expert")
     rows_out = tokens.shape[0] // n_expert
-    phi_all = lax.all_gather(phi, "expert", axis=1, tiled=True)
+    size = lax.axis_size("expert")
+    repeats = [size if d == 1 else 1 for d in range(phi.ndim)]
+    phi_all = lax.all_to_all(
+        jnp.tile(phi, repeats), "expert", split_axis=1, concat_axis=1, tiled=True
+    )
     logits = lax.dot_general(
         phi, tokens, (((0,), (1,)), ((), ())), preferred_element_type=jnp.float32
     )

time: 160 us -> 145 us (0.906)
  blocking collectives: 146 us -> 123 us
  starting transfers between devices: 0 us -> 7.03 us
    all_gather x1 -> x0, blocking collectives: 24 us -> none  [on_device(): phi_all = lax.all_gather(phi, 'expert', axis=1, tiled=True)]
    all_to_all x0 -> x1, starting transfers between devices: none -> 7.03 us  [on_device(): lax.all_to_all(jnp.tile(phi, repeats), 'expert', split_axis=1, concat_axi...]
  transfers between devices with their start and end apart: 0 -> 1, of which waited for: 0 -> 0; matrix products, arithmetic and copies ran while one was open for 0% -> 8% of each run, Pallas kernels for 0% -> 0%
where the time goes in v2:
time: 145 us
  blocking collectives  123 us (85%)
  matrix products  13.2 us (9%)
  starting transfers between devices  7.03 us (5%)
  local copies, waits for them, and re-layouts  1.5 us (1%)
    psum x1, blocking collectives, on_device(): totals = lax.psum(partial_value, ('dp', 'seq'))  51.1 us
    psum x1, blocking collectives, on_device(): numer_seq, denom_seq = lax.psum((numerator, denominator), 'seq')  27.9 us
    all_gather x1, blocking collectives, on_device(): lax.all_gather(summed.astype(jnp.bfloat16), 'expert', axis=0, tiled=True)  24.1 us
    pmax x1, blocking collectives, on_device(): slot_max = lax.pmax(jnp.max(logits, axis=1), 'seq')  17.9 us
    all_to_all x1, starting transfers between devices, on_device(): lax.all_to_all(jnp.tile(phi, repeats), 'expert', split_axis=1, concat_axi...  7.03 us
    dot_general x1, matrix products, on_device(): jnp.einsum('cef,efd->ced', hidden, w_out, preferred_element_type=jnp.floa...  4.65 us
    dot_general x1, matrix products, on_device(): lax.dot_general(phi, tokens, (((0,), (1,)), ((), ())), preferred_element_...  3.5 us
  transfers between devices with their start and end apart: 1, of which 0 were waited for; matrix products, arithmetic and copies ran while one was open for 8% of the time, Pallas kernels for 0%

profile of v2, /device:TPU:32, one launch (start us, length us, event | category | flops | bytes accessed | tf_op | source)
XLA Modules:
  0.0 144.9 jit_solution(16936149974012020730)
XLA Ops:
  0.0 1.4 tile.2
  1.4 7.0 %all-to-all-start = ((bf16[2048,16,2]{0,2,1:T(2,128)(2,1)}), bf16[2048,16,2]{0,2,1:T(2,128)(2,1)S(1)}, u32[]{:S(2)}, u32[]{:S(2)}) async-start(bf16[2048,16,2]{0,2,1:T(2,128)(2,1)} %tile.2), calls=%async_computation | async-start | bytes 262144 | tf_op jit(solution)/shard_map/all_to_all | solution.py:12
  8.5 3.5 %fusion.39 = (f32[2]{0:T(128)S(1)}, f32[2,1024]{1,0:T(2,128)S(1)}) fusion(bf16[2048,2]{0,1:T(2,128)(2,1)} %param.5, bf16[1024,2048]{1,0:T(8,128)(2,1)} %param.4), kind=kOutput, calls=%fused_computation.39 | convolution fusion | flops 8390654 | bytes 4210696 | tf_op jit(solution)/shard_map/dot_general | solution.py:15
  12.0 17.9 %pmax.7 = f32[2]{0:T(128)S(1)} all-reduce(f32[2]{0:T(128)S(1)} %get-tuple-element.9), channel_id=1, replica_groups=mesh['dp'=2,'seq'=8,'expert'=16] {'seq'}, use_global_device_ids=true, to_apply=%region_2.0 | all-reduce | flops 2 | bytes 16 | tf_op jit(solution)/shard_map/pmax | solution.py:18
  29.9 0.2 fusion.25
  30.1 2.9 %fusion.27 = f32[2,2048]{1,0:T(2,128)S(1)} fusion(bf16[1024,2048]{1,0:T(8,128)(2,1)} %param.4, f32[2,1024]{1,0:T(2,128)S(1)} %get-tuple-element.10, f32[2]{0:T(128)S(1)} %pmax.7), kind=kOutput, calls=%fused_computation.28 | convolution fusion | flops 8392704 | bytes 4218888 | tf_op jit(solution)/shard_map/dot_general | solution.py:20
  32.9 27.9 %all-reduce = (f32[2,2048]{1,0:T(2,128)S(1)}, f32[2]{0:T(128)S(1)}) all-reduce(f32[2,2048]{1,0:T(2,128)S(1)} %fusion.27, f32[2]{0:T(128)S(1)} %fusion.25), channel_id=1, replica_groups=mesh['dp'=2,'seq'=8,'expert'=16] {'seq'}, use_global_device_ids=true, to_apply=%region_3.0 | all-reduce | flops 4098 | bytes 32784 | tf_op jit(solution)/shard_map/psum | solution.py:22
  60.9 0.1 fusion.24
  60.9 1.8 %all-gather.2 = bf16[2,2,2048]{2,1,0:T(2,128)(2,1)S(1)} all-gather(bf16[1,2,2048]{2,1,0:T(2,128)(2,1)S(1)} %fusion.24), channel_id=2, replica_groups=mesh['dp'=2,'seq'=8,'expert'=16] {'dp'}, dimensions={0}, use_global_device_ids=true | all-gather | bytes 24576 | tf_op jit(solution)/shard_map/all_gather | solution.py:24
  62.7 4.7 %convolution_bitcast_fusion = f32[2,2,2048]{2,0,1:T(2,128)S(1)} fusion(bf16[2,512,2048]{2,1,0:T(8,128)(2,1)} %param.7, bf16[2,2048,512]{2,1,0:T(8,128)(2,1)} %param.6, bf16[2,2,2048]{2,1,0:T(2,128)(2,1)S(1)} %all-gather.2), kind=kOutput, calls=%fused_computation.2 | convolution fusion | flops 16795648 | bytes 8437760 | tf_op jit(solution)/shard_map/cef,efd->ced/dot_general | solution.py:29
  67.4 51.1 %psum.23 = bf16[2,2,2048]{2,0,1:T(2,128)(2,1)S(1)} all-reduce(f32[2,2,2048]{2,0,1:T(2,128)S(1)} %convolution_bitcast_fusion), channel_id=1, replica_groups=mesh['dp'=2,'seq'=8,'expert'=16] {'dp','seq'}, use_global_device_ids=true, to_apply=%region_6.7 | all-reduce | flops 8192 | bytes 49152 | tf_op jit(solution)/shard_map/psum | solution.py:30
  118.5 24.1 %all-gather.1 = bf16[1,32,2048]{2,0,1:T(2,128)(2,1)S(1)} all-gather(bf16[1,2,2048]{2,0,1:T(2,128)(2,1)S(1)} %dynamic-slice_convert_fusion), channel_id=3, replica_groups=mesh['dp'=2,'seq'=8,'expert'=16] {'expert'}, dimensions={1}, use_global_device_ids=true | all-gather | bytes 139264 | tf_op jit(solution)/shard_map/all_gather | solution.py:32
  142.6 0.0 all-to-all-done
  142.6 0.1 all_to_all.7
  142.7 1.2 fusion.38
  143.9 1.0 fusion
  (2 shorter events, 0.1 us)
Async XLA Ops:
  1.4 141.2 %all-to-all-start = ((bf16[2048,16,2]{0,2,1:T(2,128)(2,1)}), bf16[2048,16,2]{0,2,1:T(2,128)(2,1)S(1)}, u32[]{:S(2)}, u32[]{:S(2)}) async-start(bf16[2048,16,2]{0,2,1:T(2,128)(2,1)} %tile.2), calls=%async_computation | async-start | bytes 262144 | tf_op jit(solution)/shard_map/all_to_all | solution.py:12

commit v3 on v0

--- a/solution.py
+++ b/solution.py
@@ -25,7 +25,12 @@
     partial_value = jnp.einsum("cef,efd->ced", hidden, w_out, preferred_element_type=jnp.float32)
     totals = lax.psum(partial_value, ("dp", "seq"))
     summed = lax.dynamic_index_in_dim(totals, lax.axis_index("dp"), 0, keepdims=False)
-    slot_out = lax.all_gather(summed.astype(jnp.bfloat16), "expert", axis=0, tiled=True)
+    slot_out = jnp.concatenate(
+        lax.all_to_all(
+            jnp.stack([summed.astype(jnp.bfloat16)] * lax.axis_size("expert")), "expert", 0, 0
+        ),
+        axis=0,
+    )
     rows = lax.dynamic_slice_in_dim(tokens, lax.axis_index("expert") * rows_out, rows_out, 0)
     row_logits = lax.dot_general(
         phi_all, rows, (((0,), (1,)), ((), ())), preferred_element_type=jnp.float32

time: 160 us -> 145 us (0.906)
  blocking collectives: 146 us -> 123 us
  starting transfers between devices: 0 us -> 7.03 us
    all_gather x1 -> x0, blocking collectives: 23.1 us -> none  [on_device(): lax.all_gather(summed.astype(jnp.bfloat16), 'expert', axis=0, tiled=True)]
    all_to_all x0 -> x1, starting transfers between devices: none -> 7.03 us  [on_device(): lax.all_to_all(jnp.stack([summed.astype(jnp.bfloat16)] * lax.axis_size('e...]
  transfers between devices with their start and end apart: 0 -> 1, of which waited for: 0 -> 0; matrix products, arithmetic and copies ran while one was open for 0% -> 1% of each run, Pallas kernels for 0% -> 0%
where the time goes in v3:
time: 145 us; the launch traced here: 144 us
  blocking collectives  123 us (85%)
  matrix products  13.2 us (9%)
  starting transfers between devices  7.03 us (5%)
    psum x1, blocking collectives, on_device(): totals = lax.psum(partial_value, ('dp', 'seq'))  51.1 us
    psum x1, blocking collectives, on_device(): numer_seq, denom_seq = lax.psum((numerator, denominator), 'seq')  27.9 us
    all_gather x1, blocking collectives, on_device(): phi_all = lax.all_gather(phi, 'expert', axis=1, tiled=True)  24.1 us
    pmax x1, blocking collectives, on_device(): slot_max = lax.pmax(jnp.max(logits, axis=1), 'seq')  17.9 us
    all_to_all x1, starting transfers between devices, on_device(): lax.all_to_all(jnp.stack([summed.astype(jnp.bfloat16)] * lax.axis_size('e...  7.03 us
    dot_general x1, matrix products, on_device(): jnp.einsum('cef,efd->ced', hidden, w_out, preferred_element_type=jnp.floa...  4.66 us
    dot_general x1, matrix products, on_device(): lax.dot_general(phi, tokens, (((0,), (1,)), ((), ())), preferred_element_...  3.5 us
  transfers between devices with their start and end apart: 1, of which 0 were waited for; matrix products, arithmetic and copies ran while one was open for 1% of the time, Pallas kernels for 0%

profile of v3, /device:TPU:32, one launch (start us, length us, event | category | flops | bytes accessed | tf_op | source)
XLA Modules:
  0.0 144.3 jit_solution(3198205607291277104)
XLA Ops:
  0.0 3.5 %fusion.36 = (f32[2]{0:T(128)S(1)}, f32[2,1024]{1,0:T(2,128)S(1)}) fusion(bf16[2048,2]{0,1:T(2,128)(2,1)} %param.5, bf16[1024,2048]{1,0:T(8,128)(2,1)} %param.4), kind=kOutput, calls=%fused_computation.37 | convolution fusion | flops 8390654 | bytes 4210696 | tf_op jit(solution)/shard_map/dot_general | solution.py:11
  3.5 17.9 %pmax.7 = f32[2]{0:T(128)S(1)} all-reduce(f32[2]{0:T(128)S(1)} %get-tuple-element.7), channel_id=1, replica_groups=mesh['dp'=2,'seq'=8,'expert'=16] {'seq'}, use_global_device_ids=true, to_apply=%region_2.0 | all-reduce | flops 2 | bytes 16 | tf_op jit(solution)/shard_map/pmax | solution.py:14
  21.4 0.2 fusion.23
  21.6 2.9 %fusion.25 = f32[2,2048]{1,0:T(2,128)S(1)} fusion(bf16[1024,2048]{1,0:T(8,128)(2,1)} %param.4, f32[2,1024]{1,0:T(2,128)S(1)} %get-tuple-element.8, f32[2]{0:T(128)S(1)} %pmax.7), kind=kOutput, calls=%fused_computation.27 | convolution fusion | flops 8392704 | bytes 4218888 | tf_op jit(solution)/shard_map/dot_general | solution.py:16
  24.5 27.9 %all-reduce = (f32[2,2048]{1,0:T(2,128)S(1)}, f32[2]{0:T(128)S(1)}) all-reduce(f32[2,2048]{1,0:T(2,128)S(1)} %fusion.25, f32[2]{0:T(128)S(1)} %fusion.23), channel_id=1, replica_groups=mesh['dp'=2,'seq'=8,'expert'=16] {'seq'}, use_global_device_ids=true, to_apply=%region_3.0 | all-reduce | flops 4098 | bytes 32784 | tf_op jit(solution)/shard_map/psum | solution.py:18
  52.4 0.1 fusion.22
  52.5 1.8 %all-gather.2 = bf16[2,2,2048]{2,1,0:T(2,128)(2,1)S(1)} all-gather(bf16[1,2,2048]{2,1,0:T(2,128)(2,1)S(1)} %fusion.22), channel_id=2, replica_groups=mesh['dp'=2,'seq'=8,'expert'=16] {'dp'}, dimensions={0}, use_global_device_ids=true | all-gather | bytes 24576 | tf_op jit(solution)/shard_map/all_gather | solution.py:20
  54.3 0.0 copy-start
  54.3 4.7 %convolution_bitcast_fusion = f32[2,2,2048]{2,0,1:T(2,128)S(1)} fusion(bf16[2,512,2048]{2,1,0:T(8,128)(2,1)} %param.7, bf16[2,2048,512]{2,1,0:T(8,128)(2,1)} %param.6, bf16[2,2,2048]{2,1,0:T(2,128)(2,1)S(1)} %all-gather.2), kind=kOutput, calls=%fused_computation.2 | convolution fusion | flops 16795648 | bytes 8437760 | tf_op jit(solution)/shard_map/cef,efd->ced/dot_general | solution.py:25
  59.0 51.1 %psum.23 = bf16[2,2,2048]{2,0,1:T(2,128)(2,1)S(1)} all-reduce(f32[2,2,2048]{2,0,1:T(2,128)S(1)} %convolution_bitcast_fusion), channel_id=1, replica_groups=mesh['dp'=2,'seq'=8,'expert'=16] {'dp','seq'}, use_global_device_ids=true, to_apply=%region_6.7 | all-reduce | flops 8192 | bytes 49152 | tf_op jit(solution)/shard_map/psum | solution.py:26
  110.1 0.7 stack.5
  110.8 7.0 %all-to-all-start = ((bf16[16,2,2048]{2,1,0:T(2,128)(2,1)}), bf16[16,2,2048]{2,1,0:T(2,128)(2,1)S(1)}, u32[]{:S(2)}, u32[]{:S(2)}) async-start(bf16[16,2,2048]{2,1,0:T(2,128)(2,1)} %stack.5), calls=%async_computation | async-start | bytes 262144 | tf_op jit(solution)/shard_map/all_to_all | solution.py:29
  117.9 0.0 copy-done
  117.9 24.1 %all-gather.1 = bf16[16,2,2048]{2,1,0:T(2,128)(2,1)S(1)} all-gather(bf16[1,2,2048]{2,1,0:T(2,128)(2,1)S(1)} %bitcast.25), channel_id=1, replica_groups=mesh['dp'=2,'seq'=8,'expert'=16] {'expert'}, dimensions={0}, use_global_device_ids=true | all-gather | bytes 139264 | tf_op jit(solution)/shard_map/all_gather | solution.py:10
  142.0 0.1 reshape.11
  142.0 1.2 fusion.37
  143.2 0.0 all-to-all-done
  143.2 0.1 reshape.8
  143.3 1.0 fusion
  (3 shorter events, 0.1 us)
Async XLA Ops:
  54.3 63.6 %copy-start = (bf16[2048,2]{0,1:T(2,128)(2,1)S(1)}, bf16[2048,2]{0,1:T(2,128)(2,1)}, u32[]{:S(2)}) copy-start(bf16[2048,2]{0,1:T(2,128)(2,1)} %param.5) | copy-start | bytes 24580
  110.8 32.4 %all-to-all-start = ((bf16[16,2,2048]{2,1,0:T(2,128)(2,1)}), bf16[16,2,2048]{2,1,0:T(2,128)(2,1)S(1)}, u32[]{:S(2)}, u32[]{:S(2)}) async-start(bf16[16,2,2048]{2,1,0:T(2,128)(2,1)} %stack.5), calls=%async_computation | async-start | bytes 262144 | tf_op jit(solution)/shard_map/all_to_all | solution.py:29
